TPU v7x, 32 devices: a whole 2x2x4 slice. The times are simulated.
32 devices in a mesh: ctx: 16 (over z, x, core), head: 2 (over y).
Axes of the slice: x: 2, y: 2, z: 4, core: 2. Of those that a mesh axis runs over, the one named last changes fastest.
Arguments:
- q_nope: bfloat16 [2048, 16384], P('ctx', 'head'), may hold values from -6 to 6
- q_rope: bfloat16 [2048, 8192], P('ctx', 'head'), may hold values from -32 to 32
- latent: bfloat16 [2048, 576], P(('ctx', 'head')), may hold values from -32 to 32
- block_start: int32 [32], replicated, may hold values from 0 to 1984, as said below
- w_uk: bfloat16 [128, 128, 512], P('head'), may hold values from -0.5 to 0.5
- w_uv: bfloat16 [128, 512, 128], P('head'), may hold values from -1.5 to 1.5
Outputs:
- attn_out: bfloat16 [2048, 16384], P('ctx', 'head')
Inputs may be any that keep to these rules, and one draw needn't show every extreme that they name: `block_start`: blocks 2 i and 2 i + 1 start at k * 64 and (31 - k) * 64 for a k that takes each value 0 to 15 once over i.
All inputs are finite; a program needn't handle non-finite values.
Results may differ from a plain program's by a relative error of at most 0.0065.
Values may be sent and summed in bfloat16 or wider, within the bound.
A program may use at most 192 MiB of HBM per device.

v0:
```python
import functools
import math

import jax
import jax.numpy as jnp
from jax import lax
from jax.experimental import pallas as pl
from jax.experimental.pallas import tpu as pltpu
from jax.sharding import PartitionSpec as P

CHUNK = 256
LANES = 128
GROUP = 16
UNIT = 8
MESH = pl.DeviceIdType.MESH


def attention_kernel(
    scale2,
    blk,
    starts_ref,
    lat_ref,
    q_ref,
    wuv_ref,
    out_ref,
    lat_s,
    sc_s,
    acc_s,
    max_s,
    top_s,
    sum_s,
):
    group, width, value = wuv_ref.shape
    rows = group * blk
    seq, full = lat_ref.shape
    steps = seq // CHUNK + 1
    padded = lat_s.shape[1]
    me = lax.axis_index("ctx")
    start_a = starts_ref[2 * me]
    start_b = starts_ref[2 * me + 1]
    count_a = start_a // CHUNK + 1
    step = pl.program_id(0)
    last = pl.num_programs(0) - 1

    @pl.when(step == 0)
    def _():
        max_s[...] = jnp.full(max_s.shape, -1e30, jnp.float32)
        sum_s[...] = jnp.zeros(sum_s.shape, jnp.float32)
        acc_s[...] = jnp.zeros(acc_s.shape, jnp.float32)

        def place(b, _):
            src = pl.ds(pl.multiple_of(b * blk, blk), blk)
            dst = pl.ds(pl.multiple_of(starts_ref[b], blk), blk)
            lat_s[dst, :width] = lat_ref[src, :width]
            tail = lat_ref[src, width:]
            fill = jnp.zeros((blk, padded - full), tail.dtype)
            lat_s[dst, width:] = jnp.concatenate([tail, fill], axis=1)
            return 0

        lax.fori_loop(0, seq // blk, place, 0)

    def locate(t):
        upper = t >= count_a
        half = jnp.where(upper, 1, 0)
        chunk = jnp.where(upper, t - count_a, t)
        offset = jnp.where(upper, start_b, start_a) - chunk * CHUNK
        return half, pl.ds(pl.multiple_of(chunk * CHUNK, CHUNK), CHUNK), offset

    def weigh(t):
        half, keys, _ = locate(t)
        top = top_s[half]
        total = sum_s[half]
        pieces = []
        for j in range(CHUNK // LANES):
            w = jnp.exp2((sc_s[t, :, j * LANES : (j + 1) * LANES] - top) * scale2)
            total = total + w
            pieces.append(w.astype(lat_s.dtype))
        sum_s[half] = total
        acc_s[half] += jnp.dot(
            jnp.concatenate(pieces, axis=1),
            lat_s[keys, :width],
            preferred_element_type=jnp.float32,
        )

    def score(t):
        half, keys, offset = locate(t)
        s = lax.dot_general(
            q_ref[half], lat_s[keys, :], (((1,), (1,)), ((), ())), preferred_element_type=jnp.float32
        )
        row = lax.broadcasted_iota(jnp.int32, (rows, CHUNK), 0) % blk
        col = lax.broadcasted_iota(jnp.int32, (rows, CHUNK), 1)
        s = jnp.where(col - row <= offset, s, -1e30)
        sc_s[t] = s
        top = max_s[half]
        for j in range(CHUNK // LANES):
            top = jnp.maximum(top, s[:, j * LANES : (j + 1) * LANES])
        max_s[half] = top

    def run(*works):
        def body(t, _):
            for work in works:
                work(t)
            return 0

        lax.fori_loop(0, steps, body, 0)

    @pl.when(step == 0)
    def _():
        run(score)

    @pl.when(jnp.logical_and(step > 0, step < last))
    def _():
        run(weigh, score)

    @pl.when(step == last)
    def _():
        run(weigh)

    @pl.when(step > 0)
    def _():
        for h in range(group):
            own = slice(h * blk, (h + 1) * blk)
            mixed = []
            for half in range(2):
                total = jnp.sum(sum_s[half, own], axis=1, keepdims=True)
                mixed.append((acc_s[half, own] / total).astype(lat_s.dtype))
                sum_s[half, own] = jnp.zeros((blk, LANES), jnp.float32)
                acc_s[half, own] = jnp.zeros((blk, width), jnp.float32)
            out_ref[:, h * value : (h + 1) * value] = jnp.dot(
                jnp.concatenate(mixed, axis=0), wuv_ref[h], preferred_element_type=jnp.float32
            ).astype(out_ref.dtype)

    for half in range(2):
        top_s[half] = jnp.broadcast_to(
            jnp.max(max_s[half], axis=1, keepdims=True), max_s.shape[1:]
        )
        max_s[half] = jnp.full(max_s.shape[1:], -1e30, jnp.float32)


def gather_kernel(
    sizes,
    lat_ref,
    qn_ref,
    qr_ref,
    wuk_ref,
    out_ref,
    query_ref,
    qn_s,
    qr_s,
    wuk_s,
    query_s,
    own_sem,
    send_sem,
    recv_sem,
    in_sem,
    out_sem,
):
    outer, inner, heads = sizes
    _, _, rows, padded = query_s.shape
    tok = qn_s.shape[0]
    blk = tok // 2
    total, nope, width = wuk_s.shape
    group = min(UNIT, total)
    parts = total // group
    share = rows // (group * blk)
    rope = qr_s.shape[1] // total
    loads = [
        pltpu.make_async_copy(qn_ref, qn_s, in_sem.at[parts]),
        pltpu.make_async_copy(qr_ref, qr_s, in_sem.at[parts + 1]),
    ]
    for g in range(parts):
        span = pl.ds(g * group, group)
        loads.append(pltpu.make_async_copy(wuk_ref.at[span], wuk_s.at[span], in_sem.at[g]))
    stores = []
    for g in range(parts):
        at = (g // share, slice(None), pl.ds((g % share) * group * blk, group * blk))
        stores.append(pltpu.make_async_copy(query_s.at[at], query_ref.at[at], out_sem.at[g]))

    def project(g):
        if g == 0:
            loads[0].wait()
            loads[1].wait()
        if g < parts:
            loads[2 + g].wait()

            def pair(p, _):
                turns = qr_s[:, pl.ds(pl.multiple_of((g * group + 2 * p) * rope, 2 * rope), 2 * rope)]
                for j in range(2):
                    h = 2 * p + j
                    head = g * group + h
                    own = jnp.dot(
                        qn_s[:, pl.ds(pl.multiple_of(head * nope, nope), nope)],
                        wuk_s[head],
                        preferred_element_type=jnp.float32,
                    ).astype(query_s.dtype)
                    turn = turns[:, j * rope : (j + 1) * rope]
                    fill = jnp.zeros((tok, padded - width - rope), turn.dtype)
                    tail = jnp.concatenate([turn, fill], axis=1)
                    for half in range(2):
                        cut = slice(half * blk, (half + 1) * blk)
                        to = pl.ds(pl.multiple_of(((g % share) * group + h) * blk, blk), blk)
                        query_s[g // share, half, to, :width] = own[cut]
                        query_s[g // share, half, to, width:] = tail[cut]
                return 0

            lax.fori_loop(0, group // 2, pair, 0)
        if 1 <= g <= parts:
            stores[g - 1].start()

    swap = inner == heads
    me, y = lax.axis_index("ctx"), lax.axis_index("head")
    core = me % 2
    z, x = (me // 2) // inner, (me // 2) % inner
    turned = core if swap else 0
    u, v = x + turned * (y - x), y + turned * (x - y)

    def coords(zz, uu, vv):
        return zz, uu + turned * (vv - uu), vv + turned * (uu - vv)

    def block(zz, uu, vv, cc):
        zz, xx, yy = coords(zz, uu, vv)
        return ((zz * inner + xx) * 2 + cc) * heads + yy

    def device(zz, uu, vv, cc):
        zz, xx, yy = coords(zz, uu, vv)
        return ((zz * inner + xx) * 2 + cc, yy)

    zs = [(z + d) % outer for d in range(outer)]
    us = [(u + d) % inner for d in range(inner)]
    vs = [(v + d) % heads for d in range(heads)]
    z_peers = [device(p, u, v, core) for p in zs[:0:-1]]
    u_peers = [device(z, p, v, core) for p in us[1:]]
    v_peers = [device(z, u, p, core) for p in vs[1:]]
    partner = [(z * inner * 2 + x * 2 + 1 - core, y)]
    everyone = z_peers + u_peers + v_peers + partner

    own = block(z, u, v, core)
    keep = pltpu.make_async_copy(lat_ref, out_ref.at[own], own_sem)
    keep.start()
    for load in loads:
        load.start()

    barrier = pltpu.get_barrier_semaphore()
    for peer in everyone:
        pl.semaphore_signal(barrier, inc=1, device_id=peer, device_id_type=MESH)
    pl.semaphore_wait(barrier, len(everyone))

    sent = []

    def send(src, b, peers):
        for peer in peers:
            copy = pltpu.make_async_remote_copy(
                src_ref=src,
                dst_ref=out_ref.at[b],
                send_sem=send_sem.at[len(sent)],
                recv_sem=recv_sem.at[b],
                device_id=peer,
                device_id_type=MESH,
            )
            copy.start()
            sent.append(copy)

    def arrive(b):
        pltpu.make_async_remote_copy(
            src_ref=out_ref.at[b],
            dst_ref=out_ref.at[b],
            send_sem=send_sem.at[0],
            recv_sem=recv_sem.at[b],
            device_id=partner[0],
            device_id_type=MESH,
        ).wait_recv()

    def relay(b, peers):
        arrive(b)
        send(out_ref.at[b], b, peers)

    send(lat_ref, own, u_peers + v_peers + z_peers + partner)
    route = [(block(z, uu, v, core), v_peers + partner) for uu in us[1:]]
    for d in range(1, outer + 1):
        if d < outer:
            route.append((block(zs[d], u, v, core), u_peers + v_peers + partner))
        if d > 1:
            route += [(block(zs[d - 1], uu, v, core), v_peers + partner) for uu in us[1:]]
    route += [(block(zz, u, vv, core), partner) for zz in zs for vv in vs[1:]]
    route += [
        (block(zz, uu, vv, core), partner) for zz in zs for uu in us[1:] for vv in vs[1:]
    ]
    project(0)
    project(1)
    for place, (b, peers) in enumerate(route):
        relay(b, peers)
        if place % 2:
            project(2 + place // 2)
    for g in range(2 + len(route) // 2, parts + 1):
        project(g)
    for zz in range(outer):
        for xx in range(inner):
            for yy in range(heads):
                arrive(((zz * inner + xx) * 2 + 1 - core) * heads + yy)
    for copy in sent:
        copy.wait_send()
    for store in stores:
        store.wait()
    keep.wait()


def gather(latent, q_nope, q_rope, w_uk, ctx, head_axis, group):
    chips = ctx // 2
    inner = 2 if chips % 2 == 0 else 1
    sizes = (chips // inner, inner, head_axis)
    shard, full = latent.shape
    blocks = ctx * head_axis
    heads, nope, width = w_uk.shape
    tok = q_nope.shape[0]
    rows = group * tok // 2
    parts = heads // group
    padded = -(-full // LANES) * LANES
    kind = latent.dtype
    lat, query = pl.pallas_call(
        functools.partial(gather_kernel, sizes),
        out_shape=(
            jax.ShapeDtypeStruct((blocks, shard, full), kind),
            jax.ShapeDtypeStruct((parts, 2, rows, padded), kind),
        ),
        in_specs=[
            pl.BlockSpec(memory_space=pltpu.VMEM),
            pl.BlockSpec(memory_space=pl.ANY),
            pl.BlockSpec(memory_space=pl.ANY),
            pl.BlockSpec(memory_space=pl.ANY),
        ],
        out_specs=(
            pl.BlockSpec(memory_space=pltpu.VMEM),
            pl.BlockSpec(memory_space=pl.ANY),
        ),
        scratch_shapes=[
            pltpu.VMEM(q_nope.shape, kind),
            pltpu.VMEM(q_rope.shape, kind),
            pltpu.VMEM(w_uk.shape, kind),
            pltpu.VMEM((parts, 2, rows, padded), kind),
            pltpu.SemaphoreType.DMA,
            pltpu.SemaphoreType.DMA((blocks,)),
            pltpu.SemaphoreType.DMA((blocks,)),
            pltpu.SemaphoreType.DMA((heads // min(UNIT, heads) + 2,)),
            pltpu.SemaphoreType.DMA((heads // min(UNIT, heads),)),
        ],
        compiler_params=pltpu.CompilerParams(collective_id=0, has_side_effects=True),
    )(latent, q_nope, q_rope, w_uk)
    return lat.reshape(blocks * shard, full), query


def attend(lat, query, starts, w_uv, scale2, group):
    heads, width, value = w_uv.shape
    parts, _, rows, padded = query.shape
    blk = rows // group
    seq = lat.shape[0]
    steps = seq // CHUNK + 1
    return pl.pallas_call(
        functools.partial(attention_kernel, scale2, blk),
        grid=(parts + 1,),
        out_shape=jax.ShapeDtypeStruct((2 * blk, heads * value), lat.dtype),
        in_specs=[
            pl.BlockSpec(memory_space=pltpu.SMEM),
            pl.BlockSpec(memory_space=pltpu.VMEM),
            pl.BlockSpec((None, 2, rows, padded), lambda i: (jnp.minimum(i, parts - 1), 0, 0, 0)),
            pl.BlockSpec((group, width, value), lambda i: (jnp.maximum(i - 1, 0), 0, 0)),
        ],
        out_specs=pl.BlockSpec((2 * blk, group * value), lambda i: (0, jnp.maximum(i - 1, 0))),
        scratch_shapes=[
            pltpu.VMEM((seq, padded), lat.dtype),
            pltpu.VMEM((steps, rows, CHUNK), jnp.float32),
            pltpu.VMEM((2, rows, width), jnp.float32),
            pltpu.VMEM((2, rows, LANES), jnp.float32),
            pltpu.VMEM((2, rows, LANES), jnp.float32),
            pltpu.VMEM((2, rows, LANES), jnp.float32),
        ],
        compiler_params=pltpu.CompilerParams(dimension_semantics=("arbitrary",)),
    )(starts, lat, query, w_uv)


def shards(sizes, q_nope, q_rope, latent, block_start, w_uk, w_uv):
    group = min(GROUP, w_uk.shape[0])
    rope = q_rope.shape[1] // w_uk.shape[0]
    scale2 = math.log2(math.e) / math.sqrt(w_uk.shape[1] + rope)
    lat, query = gather(latent, q_nope, q_rope, w_uk, *sizes, group)
    return attend(lat, query, block_start, w_uv, scale2, group)


def solution(mesh):
    placed = (
        P("ctx", "head"),
        P("ctx", "head"),
        P(("ctx", "head"), None),
        P(),
        P("head", None, None),
        P("head", None, None),
    )
    sizes = (mesh.shape["ctx"], mesh.shape["head"])
    return jax.shard_map(
        functools.partial(shards, sizes), mesh=mesh, in_specs=placed, out_specs=P("ctx", "head"), check_vma=False
    )
```

profile of v0, /device:TPU:0, one launch (start us, length us, event | category | flops | bytes accessed | tf_op | source)
XLA Modules:
  0.0 71.1 jit_solution(774371294382352863)
XLA Ops:
  0.0 27.7 %shard_map.64 = (bf16[32,64,576]{2,1,0:T(8,128)(2,1)}, bf16[4,2,1024,640]{3,2,1,0:T(8,128)(2,1)}) custom-call(bf16[64,576]{1,0:T(8,128)(2,1)} %lat_ref.1, bf16[128,8192]{1,0:T(8,128)(2,1)} %qn_ref.1, bf16[128,4096]{1,0:T(8,128)(2,1)} %qr_ref.1, bf16[64,128,512]{2,1,0:T(8,128)(2,1)} %wuk_ref.1), custom_call_target="tpu_custom_call" | custom-call | tf_op jit(solution)/shard_map/pallas_call | solution.py:319
  27.7 43.4 %shard_map.65 = bf16[128,8192]{1,0:T(8,128)(2,1)} custom-call(s32[32]{0:T(128)} %starts_ref.1, bf16[2048,576]{1,0:T(8,128)(2,1)} %bitcast.1, bf16[4,2,1024,640]{3,2,1,0:T(8,128)(2,1)} %get-tuple-element.8.q_ref, bf16[64,512,128]{2,1,0:T(8,128)(2,1)} %wuv_ref.1), custom_call_target="tpu_custom_call" | custom-call | tf_op jit(solution)/shard_map/pallas_call | solution.py:357
where the time goes:
time: 71.2 us; the launch traced here: 71.1 us
  Pallas kernels  71.1 us (100%)
    pallas_call x1, Pallas kernels, attend(): pl.pallas_call(functools.partial(attention_kernel, scale2, blk), grid=(pa...  43.4 us
    pallas_call x1, Pallas kernels, gather(): pl.pallas_call(functools.partial(gather_kernel, sizes), out_shape=(jax.Sh...  27.7 us

commit v1 on v0

--- a/solution.py
+++ b/solution.py
@@ -12,6 +12,7 @@
 LANES = 128
 GROUP = 16
 UNIT = 8
+TURN = 3
 MESH = pl.DeviceIdType.MESH
 
 
@@ -98,23 +99,27 @@
 
     def run(*works):
         def body(t, _):
+            for n in range(TURN):
+                for work in works:
+                    work(t * TURN + n)
+            return 0
+
+        def rest(t, _):
             for work in works:
                 work(t)
             return 0
 
-        lax.fori_loop(0, steps, body, 0)
-
-    @pl.when(step == 0)
+        lax.fori_loop(0, steps // TURN, body, 0)
+        if steps % TURN:
+            lax.fori_loop(steps - steps % TURN, steps, rest, 0)
+
+    @pl.when(step > 0)
+    def _():
+        run(weigh)
+
+    @pl.when(step < last)
     def _():
         run(score)
-
-    @pl.when(jnp.logical_and(step > 0, step < last))
-    def _():
-        run(weigh, score)
-
-    @pl.when(step == last)
-    def _():
-        run(weigh)
 
     @pl.when(step > 0)
     def _():

time: 71.2 us -> 70.1 us (0.985)
  Pallas kernels: 71.1 us -> 70 us
    pallas_call x1, Pallas kernels: 43.4 us -> 42.3 us  [attend(): pl.pallas_call(functools.partial(attention_kernel, scale2, blk), grid=(pa...]
where the time goes in v1:
time: 70.1 us; the launch traced here: 70 us
  Pallas kernels  70 us (100%)
    pallas_call x1, Pallas kernels, attend(): pl.pallas_call(functools.partial(attention_kernel, scale2, blk), grid=(pa...  42.3 us
    pallas_call x1, Pallas kernels, gather(): pl.pallas_call(functools.partial(gather_kernel, sizes), out_shape=(jax.Sh...  27.7 us

profile of v1, /device:TPU:0, one launch (start us, length us, event | category | flops | bytes accessed | tf_op | source)
XLA Modules:
  0.0 70.0 jit_solution(3057643268149604040)
XLA Ops:
  0.0 27.7 %shard_map.64 = (bf16[32,64,576]{2,1,0:T(8,128)(2,1)}, bf16[4,2,1024,640]{3,2,1,0:T(8,128)(2,1)}) custom-call(bf16[64,576]{1,0:T(8,128)(2,1)} %lat_ref.1, bf16[128,8192]{1,0:T(8,128)(2,1)} %qn_ref.1, bf16[128,4096]{1,0:T(8,128)(2,1)} %qr_ref.1, bf16[64,128,512]{2,1,0:T(8,128)(2,1)} %wuk_ref.1), custom_call_target="tpu_custom_call" | custom-call | tf_op jit(solution)/shard_map/pallas_call | solution.py:324
  27.7 42.3 %shard_map.65 = bf16[128,8192]{1,0:T(8,128)(2,1)} custom-call(s32[32]{0:T(128)} %starts_ref.1, bf16[2048,576]{1,0:T(8,128)(2,1)} %bitcast.1, bf16[4,2,1024,640]{3,2,1,0:T(8,128)(2,1)} %get-tuple-element.8.q_ref, bf16[64,512,128]{2,1,0:T(8,128)(2,1)} %wuv_ref.1), custom_call_target="tpu_custom_call" | custom-call | tf_op jit(solution)/shard_map/pallas_call | solution.py:362

commit v2 on v1

--- a/solution.py
+++ b/solution.py
@@ -12,7 +12,7 @@
 LANES = 128
 GROUP = 16
 UNIT = 8
-TURN = 3
+TURN = 9
 MESH = pl.DeviceIdType.MESH
 
 
@@ -135,11 +135,13 @@
                 jnp.concatenate(mixed, axis=0), wuv_ref[h], preferred_element_type=jnp.float32
             ).astype(out_ref.dtype)
 
-    for half in range(2):
-        top_s[half] = jnp.broadcast_to(
-            jnp.max(max_s[half], axis=1, keepdims=True), max_s.shape[1:]
-        )
-        max_s[half] = jnp.full(max_s.shape[1:], -1e30, jnp.float32)
+    @pl.when(step < last)
+    def _():
+        for half in range(2):
+            top_s[half] = jnp.broadcast_to(
+                jnp.max(max_s[half], axis=1, keepdims=True), max_s.shape[1:]
+            )
+            max_s[half] = jnp.full(max_s.shape[1:], -1e30, jnp.float32)
 
 
 def gather_kernel(

time: 70.1 us -> 68 us (0.970)
  Pallas kernels: 70 us -> 67.8 us
    pallas_call x1, Pallas kernels: 42.3 us -> 40.1 us  [attend(): pl.pallas_call(functools.partial(attention_kernel, scale2, blk), grid=(pa...]
where the time goes in v2:
time: 68 us; the launch traced here: 67.8 us
  Pallas kernels  67.8 us (100%)
    pallas_call x1, Pallas kernels, attend(): pl.pallas_call(functools.partial(attention_kernel, scale2, blk), grid=(pa...  40.1 us
    pallas_call x1, Pallas kernels, gather(): pl.pallas_call(functools.partial(gather_kernel, sizes), out_shape=(jax.Sh...  27.7 us

profile of v2, /device:TPU:0, one launch (start us, length us, event | category | flops | bytes accessed | tf_op | source)
XLA Modules:
  0.0 67.8 jit_solution(11504158028879152825)
XLA Ops:
  0.0 27.7 %shard_map.64 = (bf16[32,64,576]{2,1,0:T(8,128)(2,1)}, bf16[4,2,1024,640]{3,2,1,0:T(8,128)(2,1)}) custom-call(bf16[64,576]{1,0:T(8,128)(2,1)} %lat_ref.1, bf16[128,8192]{1,0:T(8,128)(2,1)} %qn_ref.1, bf16[128,4096]{1,0:T(8,128)(2,1)} %qr_ref.1, bf16[64,128,512]{2,1,0:T(8,128)(2,1)} %wuk_ref.1), custom_call_target="tpu_custom_call" | custom-call | tf_op jit(solution)/shard_map/pallas_call | solution.py:326
  27.7 40.1 %shard_map.65 = bf16[128,8192]{1,0:T(8,128)(2,1)} custom-call(s32[32]{0:T(128)} %starts_ref.1, bf16[2048,576]{1,0:T(8,128)(2,1)} %bitcast.1, bf16[4,2,1024,640]{3,2,1,0:T(8,128)(2,1)} %get-tuple-element.8.q_ref, bf16[64,512,128]{2,1,0:T(8,128)(2,1)} %wuv_ref.1), custom_call_target="tpu_custom_call" | custom-call | tf_op jit(solution)/shard_map/pallas_call | solution.py:364
